TPU v7x, 32 devices: a whole 2x2x4 slice. The times are simulated.
32 devices in a mesh: dp: 16 (over z, y, core), tensor: 2 (over x).
Axes of the slice: x: 2, y: 2, z: 4, core: 2. Of those that a mesh axis runs over, the one named last changes fastest.
Arguments:
- latents: bfloat16 [16384, 1024], P(('dp', 'tensor')), may hold values from -6 to 6
- inputs: bfloat16 [65536, 1024], P(('dp', 'tensor')), may hold values from -6 to 6
- frames: int32 [128], replicated, may hold values from 4 to 16, as said below
- group_clip: int32 [128], P('dp'), may hold values from 0 to 127, each once
- norm_gain: float32 [4, 1024], replicated, may hold values from 0.5 to 1.5
- norm_bias: float32 [4, 1024], replicated, may hold values from -2 to 2
- cross_q: bfloat16 [1024, 1024], P(None, 'tensor'), may hold values from -0.1875 to 0.1875
- cross_k: bfloat16 [1024, 1024], P(None, 'tensor'), may hold values from -0.1875 to 0.1875
- cross_v: bfloat16 [1024, 1024], P(None, 'tensor'), may hold values from -0.1875 to 0.1875
- cross_o: bfloat16 [1024, 1024], P('tensor'), may hold values from -1 to 1
- self_q: bfloat16 [1024, 1024], P(None, 'tensor'), may hold values from -0.1875 to 0.1875
- self_k: bfloat16 [1024, 1024], P(None, 'tensor'), may hold values from -0.1875 to 0.1875
- self_v: bfloat16 [1024, 1024], P(None, 'tensor'), may hold values from -0.1875 to 0.1875
- self_o: bfloat16 [1024, 1024], P('tensor'), may hold values from -0.75 to 0.75
- mlp_up: bfloat16 [1024, 4096], P(None, 'tensor'), may hold values from -0.1875 to 0.1875
- up_bias: bfloat16 [4096], P('tensor'), may hold values from -3 to 3
- mlp_down: bfloat16 [4096, 1024], P('tensor'), may hold values from -0.09375 to 0.09375
- out_bias: float32 [3, 1024], replicated, may hold values from -2 to 2
- cotangent: bfloat16 [16384, 1024], P(('dp', 'tensor')), may hold values from -6 to 6
Outputs:
- result: bfloat16 [16384, 1024], P(('dp', 'tensor'))
- d_latents: float32 [16384, 1024], P(('dp', 'tensor'))
- d_inputs: float32 [65536, 1024], P(('dp', 'tensor'))
- d_norm_gain: float32 [4, 1024], replicated
- d_norm_bias: float32 [4, 1024], replicated
- d_out_bias: float32 [3, 1024], replicated
- d_cross_q: float32 [1024, 1024], P(None, 'tensor')
- d_cross_k: float32 [1024, 1024], P(None, 'tensor')
- d_cross_v: float32 [1024, 1024], P(None, 'tensor')
- d_cross_o: float32 [1024, 1024], P('tensor')
- d_self_q: float32 [1024, 1024], P(None, 'tensor')
- d_self_k: float32 [1024, 1024], P(None, 'tensor')
- d_self_v: float32 [1024, 1024], P(None, 'tensor')
- d_self_o: float32 [1024, 1024], P('tensor')
- d_mlp_up: float32 [1024, 4096], P(None, 'tensor')
- d_up_bias: float32 [4096], P('tensor')
- d_mlp_down: float32 [4096, 1024], P('tensor')
Inputs may be any that keep to these rules, and one draw needn't show every extreme that they name: Each clip has 4 or 16 frames, and both counts occur. `group_clip`: every clip index belongs to exactly one group.
All inputs are finite; a program needn't handle non-finite values.
Results may differ from a plain program's by a relative error of at most 0.03.
Values may be sent and summed in bfloat16 or wider, within the bound.
A program may use at most 256 MiB of HBM per device.

v0:
```python
import jax
import jax.numpy as jnp
from jax import lax
from jax.sharding import PartitionSpec as P

HS = 128
LAT = 128
FRAME_ROWS = 32
EPSILON = 1e-05
NEG_LARGE = -1e30
GELU_COEF = 0.7978845608028654
GELU_CUBE = 0.044715


def layer_norm(values, gain, shift):
    average = jnp.mean(values, axis=-1, keepdims=True)
    centered = values - average
    variance = jnp.mean(centered * centered, axis=-1, keepdims=True)
    return centered * lax.rsqrt(variance + EPSILON) * gain + shift


def gelu_tanh(values):
    inner = GELU_COEF * (values + GELU_CUBE * values * values * values)
    return 0.5 * values * (1.0 + jnp.tanh(inner))


def gelu_slope(values):
    squared = values * values
    hyperbolic = jnp.tanh(GELU_COEF * (values + GELU_CUBE * squared * values))
    return 0.5 * (1.0 + hyperbolic) + 0.5 * values * (1.0 - hyperbolic * hyperbolic) * GELU_COEF * (
        1.0 + 3.0 * GELU_CUBE * squared
    )


def matmul(left, right):
    return jnp.dot(left, right, preferred_element_type=jnp.float32)


def gram_left(left, right):
    return lax.dot_general(
        left, right, (((0,), (0,)), ((), ())), preferred_element_type=jnp.float32
    )


def times_transposed(left, right):
    return lax.dot_general(
        left, right, (((1,), (1,)), ((), ())), preferred_element_type=jnp.float32
    )


def block_size(groups):
    chosen = 1
    for candidate in (4, 3, 2):
        if chosen == 1 and groups % candidate == 0:
            chosen = candidate
    return chosen


def split_blocks(array, groups, head_size):
    block = block_size(groups)
    rows = array.shape[0] // groups
    heads = array.shape[1] // head_size
    return array.reshape(groups // block, block, rows, heads, head_size)


def masked_scores(query_block, key_block, length_block, head_size):
    key_count = key_block.shape[1]
    scores = jnp.einsum(
        "gqhd,gkhd->ghqk", query_block, key_block, preferred_element_type=jnp.float32
    ) * head_size ** (-0.5)
    positions = lax.broadcasted_iota(jnp.int32, (1, 1, 1, key_count), 3)
    return jnp.where(positions < length_block[:, None, None, None], scores, NEG_LARGE)


def attend_forward(queries, key_vecs, value_vecs, lengths, head_size):
    groups = lengths.shape[0]
    block = block_size(groups)
    pieces = (
        split_blocks(queries, groups, head_size),
        split_blocks(key_vecs, groups, head_size),
        split_blocks(value_vecs, groups, head_size),
        lengths.reshape(groups // block, block),
    )

    def one_block(piece):
        query_block, key_block, value_block, length_block = piece
        scores = masked_scores(query_block, key_block, length_block, head_size)
        row_max = jnp.max(scores, axis=-1, keepdims=True)
        exponent = jnp.exp(scores - row_max)
        row_total = jnp.sum(exponent, axis=-1, keepdims=True)
        probability = (exponent / row_total).astype(jnp.bfloat16)
        mixed = jnp.einsum(
            "ghqk,gkhd->gqhd", probability, value_block, preferred_element_type=jnp.float32
        )
        return (mixed.astype(jnp.bfloat16), (row_max + jnp.log(row_total))[..., 0])

    mixed, log_total = lax.map(one_block, pieces)
    return (mixed.reshape(queries.shape), log_total)


def attend_backward(queries, key_vecs, value_vecs, grad_mixed, log_total, lengths, head_size):
    groups = lengths.shape[0]
    block = block_size(groups)
    pieces = (
        split_blocks(queries, groups, head_size),
        split_blocks(key_vecs, groups, head_size),
        split_blocks(value_vecs, groups, head_size),
        split_blocks(grad_mixed, groups, head_size),
        log_total,
        lengths.reshape(groups // block, block),
    )
    scale_factor = head_size ** (-0.5)

    def one_block(piece):
        query_block, key_block, value_block, grad_block, total_block, length_block = piece
        scores = masked_scores(query_block, key_block, length_block, head_size)
        probability = jnp.exp(scores - total_block[..., None])
        grad_prob = jnp.einsum(
            "gqhd,gkhd->ghqk", grad_block, value_block, preferred_element_type=jnp.float32
        )
        inner = jnp.sum(probability * grad_prob, axis=-1, keepdims=True)
        grad_score = (probability * (grad_prob - inner)).astype(jnp.bfloat16)
        grad_query = (
            jnp.einsum("ghqk,gkhd->gqhd", grad_score, key_block, preferred_element_type=jnp.float32)
            * scale_factor
        )
        grad_key = (
            jnp.einsum(
                "ghqk,gqhd->gkhd", grad_score, query_block, preferred_element_type=jnp.float32
            )
            * scale_factor
        )
        grad_value = jnp.einsum(
            "ghqk,gqhd->gkhd",
            probability.astype(jnp.bfloat16),
            grad_block,
            preferred_element_type=jnp.float32,
        )
        return (
            grad_query.astype(jnp.bfloat16),
            grad_key.astype(jnp.bfloat16),
            grad_value.astype(jnp.bfloat16),
        )

    grad_query, grad_key, grad_value = lax.map(one_block, pieces)
    return (
        grad_query.reshape(queries.shape),
        grad_key.reshape(key_vecs.shape),
        grad_value.reshape(value_vecs.shape),
    )


def gather_rows(normed):
    return lax.all_gather(normed, "tensor", axis=0, tiled=True)


def gather_grads(grads):
    return lax.all_gather(grads, "tensor", axis=0, tiled=True)


def branch_sum(mixed, weight, own_rows):

    def term(begin_row, row_count):
        return matmul(mixed, weight)

    return lax.psum_scatter(
        term(jnp.int32(0), lax.axis_size("tensor") * own_rows),
        "tensor",
        scatter_dimension=0,
        tiled=True,
    )


def back_rows(term, own_rows):
    return lax.psum_scatter(
        term(jnp.int32(0), own_rows * lax.axis_size("tensor")).astype(jnp.bfloat16),
        "tensor",
        scatter_dimension=0,
        tiled=True,
    ).astype(jnp.float32)


def back_inputs(term, own_rows):
    return lax.psum_scatter(
        term(jnp.int32(0), own_rows * lax.axis_size("tensor")).astype(jnp.bfloat16),
        "tensor",
        scatter_dimension=0,
        tiled=True,
    ).astype(jnp.float32)


def shards(
    latents,
    inputs,
    frames,
    group_clip,
    norm_gain,
    norm_bias,
    cross_q,
    cross_k,
    cross_v,
    cross_o,
    self_q,
    self_k,
    self_v,
    self_o,
    mlp_up,
    up_bias,
    mlp_down,
    out_bias,
    cotangent,
):
    head_size = HS
    own_rows = latents.shape[0]
    own_inputs = inputs.shape[0]
    stream = latents.astype(jnp.float32)
    source = inputs.astype(jnp.float32)
    lat_normed = layer_norm(stream, norm_gain[0], norm_bias[0]).astype(jnp.bfloat16)
    in_normed = layer_norm(source, norm_gain[1], norm_bias[1]).astype(jnp.bfloat16)
    local_set = (
        cross_q,
        cross_k,
        cross_v,
        cross_o,
        self_q,
        self_k,
        self_v,
        self_o,
        mlp_up,
        up_bias,
        mlp_down,
    )
    rows_cross, rows_input = (
        lax.all_gather(lat_normed, "tensor", axis=0, tiled=True),
        lax.all_gather(in_normed, "tensor", axis=0, tiled=True),
    )
    (
        w_cross_q,
        w_cross_k,
        w_cross_v,
        w_cross_o,
        w_self_q,
        w_self_k,
        w_self_v,
        w_self_o,
        w_up,
        b_up,
        w_down,
    ) = local_set
    matches = group_clip[:, None] == lax.broadcasted_iota(jnp.int32, (1, frames.shape[0]), 1)
    lengths = jnp.sum(jnp.where(matches, frames[None, :], 0), axis=1) * FRAME_ROWS
    full_lengths = jnp.full(lengths.shape, LAT, jnp.int32)
    cross_query = matmul(rows_cross, w_cross_q).astype(jnp.bfloat16)
    cross_keys = matmul(rows_input, w_cross_k).astype(jnp.bfloat16)
    cross_values = matmul(rows_input, w_cross_v).astype(jnp.bfloat16)
    cross_mixed, cross_total = attend_forward(
        cross_query, cross_keys, cross_values, lengths, head_size
    )
    stream1 = stream + branch_sum(cross_mixed, w_cross_o, own_rows) + out_bias[0]
    self_normed = layer_norm(stream1, norm_gain[2], norm_bias[2]).astype(jnp.bfloat16)
    rows_self = gather_rows(self_normed)
    self_query = matmul(rows_self, w_self_q).astype(jnp.bfloat16)
    self_keys = matmul(rows_self, w_self_k).astype(jnp.bfloat16)
    self_values = matmul(rows_self, w_self_v).astype(jnp.bfloat16)
    self_mixed, self_total = attend_forward(
        self_query, self_keys, self_values, full_lengths, head_size
    )
    stream2 = stream1 + branch_sum(self_mixed, w_self_o, own_rows) + out_bias[1]
    mlp_normed = layer_norm(stream2, norm_gain[3], norm_bias[3]).astype(jnp.bfloat16)
    rows_mlp = gather_rows(mlp_normed)
    pre_act = matmul(rows_mlp, w_up) + b_up.astype(jnp.float32)
    hidden = gelu_tanh(pre_act).astype(jnp.bfloat16)
    stream3 = stream2 + branch_sum(hidden, w_down, own_rows) + out_bias[2]
    result = stream3.astype(jnp.bfloat16)
    grad3 = cotangent.astype(jnp.float32)
    rows_grad3 = gather_grads(grad3.astype(jnp.bfloat16))
    d_down = gram_left(hidden, rows_grad3)
    d_pre = (times_transposed(rows_grad3, w_down) * gelu_slope(pre_act)).astype(jnp.bfloat16)
    d_upb = jnp.sum(d_pre.astype(jnp.float32), axis=0)
    d_up = gram_left(rows_mlp, d_pre)
    d_mlp_rows = back_rows(lambda begin_row, row_count: times_transposed(d_pre, w_up), own_rows)
    ln_value, ln_pull = jax.vjp(layer_norm, stream2, norm_gain[3], norm_bias[3])
    d_stream2, gain_three, shift_three = ln_pull(d_mlp_rows)
    grad2 = grad3 + d_stream2
    rows_grad2 = gather_grads(grad2.astype(jnp.bfloat16))
    self_query = matmul(rows_self, w_self_q).astype(jnp.bfloat16)
    self_keys = matmul(rows_self, w_self_k).astype(jnp.bfloat16)
    self_values = matmul(rows_self, w_self_v).astype(jnp.bfloat16)
    self_mixed, self_total = attend_forward(
        self_query, self_keys, self_values, full_lengths, head_size
    )
    d_self_o = gram_left(self_mixed, rows_grad2)
    d_self_mixed = times_transposed(rows_grad2, w_self_o).astype(jnp.bfloat16)
    d_self_query, d_self_keys, d_self_values = attend_backward(
        self_query, self_keys, self_values, d_self_mixed, self_total, full_lengths, head_size
    )
    d_self_q = gram_left(rows_self, d_self_query)
    d_self_k = gram_left(rows_self, d_self_keys)
    d_self_v = gram_left(rows_self, d_self_values)

    def self_term(begin_row, row_count):
        return (
            times_transposed(d_self_query, w_self_q)
            + times_transposed(d_self_keys, w_self_k)
            + times_transposed(d_self_values, w_self_v)
        )

    d_self_rows = back_rows(self_term, own_rows)
    ln_value, ln_pull = jax.vjp(layer_norm, stream1, norm_gain[2], norm_bias[2])
    d_stream1, gain_two, shift_two = ln_pull(d_self_rows)
    grad1 = grad2 + d_stream1
    rows_grad1 = gather_grads(grad1.astype(jnp.bfloat16))
    d_cross_o = gram_left(cross_mixed, rows_grad1)
    d_cross_mixed = times_transposed(rows_grad1, w_cross_o).astype(jnp.bfloat16)
    d_cross_query, d_cross_keys, d_cross_values = attend_backward(
        cross_query, cross_keys, cross_values, d_cross_mixed, cross_total, lengths, head_size
    )
    d_cross_q = gram_left(rows_cross, d_cross_query)
    d_cross_k = gram_left(rows_input, d_cross_keys)
    d_cross_v = gram_left(rows_input, d_cross_values)
    d_lat_rows = back_rows(
        lambda begin_row, row_count: times_transposed(d_cross_query, w_cross_q), own_rows
    )

    def input_term(begin_row, row_count):
        return times_transposed(d_cross_keys, w_cross_k) + times_transposed(
            d_cross_values, w_cross_v
        )

    d_in_rows = back_inputs(input_term, own_inputs)
    ln_value, ln_pull = jax.vjp(layer_norm, stream, norm_gain[0], norm_bias[0])
    d_stream0, gain_zero, shift_zero = ln_pull(d_lat_rows)
    d_latents = grad1 + d_stream0
    ln_value, ln_pull = jax.vjp(layer_norm, source, norm_gain[1], norm_bias[1])
    d_inputs, gain_one, shift_one = ln_pull(d_in_rows)
    gain_grads = jnp.stack([gain_zero, gain_one, gain_two, gain_three])
    shift_grads = jnp.stack([shift_zero, shift_one, shift_two, shift_three])
    bias_grads = jnp.stack([jnp.sum(grad1, axis=0), jnp.sum(grad2, axis=0), jnp.sum(grad3, axis=0)])
    gain_grads, shift_grads, bias_grads = lax.psum(
        (gain_grads, shift_grads, bias_grads), ("dp", "tensor")
    )
    (
        d_cross_q,
        d_cross_k,
        d_cross_v,
        d_cross_o,
        d_self_q,
        d_self_k,
        d_self_v,
        d_self_o,
        d_up,
        d_upb,
        d_down,
    ) = (
        lax.psum(d_cross_q.astype(jnp.bfloat16), "dp").astype(jnp.float32),
        lax.psum(d_cross_k.astype(jnp.bfloat16), "dp").astype(jnp.float32),
        lax.psum(d_cross_v.astype(jnp.bfloat16), "dp").astype(jnp.float32),
        lax.psum(d_cross_o.astype(jnp.bfloat16), "dp").astype(jnp.float32),
        lax.psum(d_self_q.astype(jnp.bfloat16), "dp").astype(jnp.float32),
        lax.psum(d_self_k.astype(jnp.bfloat16), "dp").astype(jnp.float32),
        lax.psum(d_self_v.astype(jnp.bfloat16), "dp").astype(jnp.float32),
        lax.psum(d_self_o.astype(jnp.bfloat16), "dp").astype(jnp.float32),
        lax.psum(d_up.astype(jnp.bfloat16), "dp").astype(jnp.float32),
        lax.psum(d_upb.astype(jnp.bfloat16), "dp").astype(jnp.float32),
        lax.psum(d_down.astype(jnp.bfloat16), "dp").astype(jnp.float32),
    )
    return (
        result,
        d_latents,
        d_inputs,
        gain_grads,
        shift_grads,
        bias_grads,
        d_cross_q,
        d_cross_k,
        d_cross_v,
        d_cross_o,
        d_self_q,
        d_self_k,
        d_self_v,
        d_self_o,
        d_up,
        d_upb,
        d_down,
    )


def solution(mesh):
    in_specs = (
        P(("dp", "tensor"), None),
        P(("dp", "tensor"), None),
        P(),
        P("dp"),
        P(),
        P(),
        P(None, "tensor"),
        P(None, "tensor"),
        P(None, "tensor"),
        P("tensor", None),
        P(None, "tensor"),
        P(None, "tensor"),
        P(None, "tensor"),
        P("tensor", None),
        P(None, "tensor"),
        P("tensor"),
        P("tensor", None),
        P(),
        P(("dp", "tensor"), None),
    )
    out_specs = (
        P(("dp", "tensor"), None),
        P(("dp", "tensor"), None),
        P(("dp", "tensor"), None),
        P(),
        P(),
        P(),
        P(None, "tensor"),
        P(None, "tensor"),
        P(None, "tensor"),
        P("tensor", None),
        P(None, "tensor"),
        P(None, "tensor"),
        P(None, "tensor"),
        P("tensor", None),
        P(None, "tensor"),
        P("tensor"),
        P("tensor", None),
    )
    return jax.shard_map(shards, mesh=mesh, in_specs=in_specs, out_specs=out_specs, check_vma=False)
```

profile of v0, /device:TPU:0, one launch (start us, length us, event | category | flops | bytes accessed | tf_op | source)
XLA Modules:
  0.0 1340.8 jit_solution(18422580686185604196)
XLA Ops:
  24.9 26.5 %all-gather.10.cloned.1.call-done = bf16[1024,1024]{1,0:T(8,128)(2,1)} async-done(((bf16[512,1024]{1,0:T(8,128)(2,1)}), bf16[1024,1024]{1,0:T(8,128)(2,1)}) %all-gather.10.cloned.1.call-update) | async-done | bytes 2097168 | tf_op jit(solution)/shard_map/all_gather | solution.py:234
  56.0 101.6 %all-gather.8.cloned.1.call-done = bf16[4096,1024]{1,0:T(8,128)(2,1)} async-done(((bf16[2048,1024]{1,0:T(8,128)(2,1)}), bf16[4096,1024]{1,0:T(8,128)(2,1)}) %all-gather.8.cloned.1.call-update) | async-done | bytes 8388624 | tf_op jit(solution)/shard_map/all_gather | solution.py:235
  157.6 9.4 convolution_convert_fusion.3
  167.1 6.9 reshape.380
  173.9 5.3 copy.124
  179.3 9.4 convolution_convert_fusion.4
  188.7 6.9 reshape.378
  196.8 24.9 %while.62 = (s32[]{:T(128)}, bf16[2,4,128,4,128]{4,3,2,1,0:T(4,128)(2,1)}, f32[2,4,4,128]{3,2,1,0:T(4,128)S(1)}, bf16[2,4,512,4,128]{4,3,2,1,0:T(4,128)(2,1)}, s...) while((s32[]{:T(128)}, ...), condition=%wide.region_8.9_spmd, body=%wide.region_5.8_spmd.sunk | while | flops 549715968 | bytes 45163760 | solution.py:97
  221.7 4.8 fusion.191
  227.2 53.8 %reduce-scatter.8.cloned.1.call-done = f32[512,1024]{1,0:T(8,128)} async-done(((f32[1024,1024]{1,0:T(8,128)}), f32[512,1024]{1,0:T(8,128)}) %reduce-scatter.8.cloned.1.call-update) | async-done | bytes 2097168 | tf_op jit(solution)/shard_map/reduce_scatter | solution.py:166
  285.1 33.2 %all-gather.12.cloned.1.call-done = bf16[1024,1024]{1,0:T(8,128)(2,1)} async-done(((bf16[512,1024]{1,0:T(8,128)(2,1)}), bf16[1024,1024]{1,0:T(8,128)(2,1)}) %all-gather.12.cloned.1.call-update) | async-done | bytes 2097168 | tf_op jit(solution)/shard_map/all_gather | solution.py:154
  345.4 18.6 %while.63 = (s32[]{:T(128)}, bf16[2,4,128,4,128]{4,3,2,1,0:T(4,128)(2,1)}, bf16[2,4,128,4,128]{2,4,3,1,0:T(8,128)(2,1)}, bf16[2,4,128,4,128]{4,2,3,1,0:T(8,128)(...) while((s32[]{:T(128)}, bf16[2,4,128,4,128]{4,3,2,1,0:T(4,128)(2,1)}, ...), condition=%wide.region_15.16_spmd, body=%wide.region_12.15_spmd.sunk | while | flops 136053376 | bytes 6309973 | solution.py:97
  364.0 4.8 fusion.187
  368.9 54.5 %reduce-scatter.10.cloned.1.call-done = f32[512,1024]{1,0:T(8,128)} async-done(((f32[1024,1024]{1,0:T(8,128)}), f32[512,1024]{1,0:T(8,128)}) %reduce-scatter.10.cloned.1.call-update) | async-done | bytes 2097168 | tf_op jit(solution)/shard_map/reduce_scatter | solution.py:166
  429.3 32.0 %all-gather.14.cloned.1.call-done = bf16[1024,1024]{1,0:T(8,128)(2,1)} async-done(((bf16[512,1024]{1,0:T(8,128)(2,1)}), bf16[1024,1024]{1,0:T(8,128)(2,1)}) %all-gather.14.cloned.1.call-update) | async-done | bytes 2097168 | tf_op jit(solution)/shard_map/all_gather | solution.py:154
  461.3 10.9 fusion.228
  472.1 23.8 %all-gather.16.cloned.1.call-done = bf16[1024,1024]{1,0:T(8,128)(2,1)} async-done(((bf16[512,1024]{1,0:T(8,128)(2,1)}), bf16[1024,1024]{1,0:T(8,128)(2,1)}) %all-gather.16.cloned.1.call-update) | async-done | bytes 2097168 | tf_op jit(solution)/shard_map/all_gather | solution.py:158
  495.9 13.1 fusion.227
  511.0 5.7 convolution_convert_fusion.8
  517.0 11.8 fusion.211
  528.9 19.9 %reduce-scatter.14.cloned.1.call-done = bf16[512,1024]{1,0:T(8,128)(2,1)} async-done(((bf16[1024,1024]{1,0:T(8,128)(2,1)}), bf16[512,1024]{1,0:T(8,128)(2,1)}) %reduce-scatter.14.cloned.1.call-update) | async-done | bytes 1048592 | tf_op jit(solution)/shard_map/reduce_scatter | solution.py:175
  551.5 54.1 %reduce-scatter.12.cloned.1.call-done = f32[512,1024]{1,0:T(8,128)} async-done(((f32[1024,1024]{1,0:T(8,128)}), f32[512,1024]{1,0:T(8,128)}) %reduce-scatter.12.cloned.1.call-update) | async-done | bytes 2097168 | tf_op jit(solution)/shard_map/reduce_scatter | solution.py:166
  614.3 8.9 while.64
  623.2 22.8 %all-gather.18.cloned.1.call-done = bf16[1024,1024]{1,0:T(8,128)(2,1)} async-done(((bf16[512,1024]{1,0:T(8,128)(2,1)}), bf16[1024,1024]{1,0:T(8,128)(2,1)}) %all-gather.18.cloned.1.call-update) | async-done | bytes 2097168 | tf_op jit(solution)/shard_map/all_gather | solution.py:158
  656.0 22.7 %while.65 = (s32[]{:T(128)}, bf16[2,4,128,4,128]{4,3,2,1,0:T(4,128)(2,1)}, bf16[2,4,128,4,128]{4,3,2,1,0:T(4,128)(2,1)}, bf16[2,4,128,4,128]{4,3,2,1,0:T(4,128)(...) while((s32[]{:T(128)}, ...), condition=%wide.region_29.30_spmd, body=%wide.region_27.29_spmd.sunk | while | flops 339212800 | bytes 40413460 | solution.py:145
  686.3 12.6 convolution_convert_fusion.5
  698.9 19.1 %reduce-scatter.16.cloned.1.call-done = bf16[512,1024]{1,0:T(8,128)(2,1)} async-done(((bf16[1024,1024]{1,0:T(8,128)(2,1)}), bf16[512,1024]{1,0:T(8,128)(2,1)}) %reduce-scatter.16.cloned.1.call-update) | async-done | bytes 1048592 | tf_op jit(solution)/shard_map/reduce_scatter | solution.py:175
  728.3 9.6 convolution_convert_fusion.6
  744.7 16.3 %all-gather.20.cloned.1.call-done = bf16[1024,1024]{1,0:T(8,128)(2,1)} async-done(((bf16[512,1024]{1,0:T(8,128)(2,1)}), bf16[1024,1024]{1,0:T(8,128)(2,1)}) %all-gather.20.cloned.1.call-update) | async-done | bytes 2097168 | tf_op jit(solution)/shard_map/all_gather | solution.py:158
  765.6 64.0 %while.66 = (s32[]{:T(128)}, bf16[2,4,128,4,128]{4,3,2,1,0:T(4,128)(2,1)}, bf16[2,4,512,4,128]{4,3,2,1,0:T(4,128)(2,1)}, bf16[2,4,512,4,128]{4,3,2,1,0:T(4,128)(...) while((s32[]{:T(128)}, ...), condition=%wide.region_35.36_spmd, body=%wide.region_33.35_spmd.sunk | while | flops 1361575936 | bytes 150537648 | solution.py:145
  777.8 4.7 multiply_reduce_fusion.7
  791.9 5.7 constant_dynamic-update-slice_fusion.18
  797.9 4.4 constant_dynamic-slice_fusion.15
  809.8 4.7 multiply_reduce_fusion.7
  823.8 5.8 constant_dynamic-update-slice_fusion.18
  842.7 9.1 fusion.171
  851.9 5.5 fusion.168
  857.4 10.5 fusion.142
  868.0 11.4 add_convert_fusion
  880.0 35.8 %psum.110 = bf16[2048]{0:T(1024)(128)(2,1)S(1)} all-reduce(bf16[2048]{0:T(1024)(128)(2,1)S(1)} %copy-done.87), channel_id=1, replica_groups=mesh['dp'=16,'tensor'=2] {'dp'}, use_global_device_ids=true, to_apply=%region_66.67 | all-reduce | flops 2048 | bytes 8192 | tf_op jit(solution)/shard_map/psum | solution.py:364
  923.2 249.8 %all-reduce.4.cloned.1.call-done = (bf16[1024,512]{1,0:T(8,128)(2,1)}, bf16[1024,512]{1,0:T(8,128)(2,1)}, bf16[1024,512]{1,0:T(8,128)(2,1)}, bf16[512,1024]{1,0:...) async-done(((bf16[1024,512]{1,0:T(8,128)(2,1)}, ...) | async-done | bytes 16777232 | tf_op jit(solution)/shard_map/psum | solution.py:355
  1188.5 4.4 convert_element_type.277
  1193.0 4.4 convert_element_type.280
  1197.4 77.4 %reduce-scatter.20.cloned.1.call-done = bf16[2048,1024]{1,0:T(8,128)(2,1)} async-done(((bf16[4096,1024]{1,0:T(8,128)(2,1)}), bf16[2048,1024]{1,0:T(8,128)(2,1)}) %reduce-scatter.20.cloned.1.call-update) | async-done | bytes 4194320 | tf_op jit(solution)/shard_map/reduce_scatter | solution.py:184
  1274.8 5.8 convert_reduce_fusion
  1280.8 5.4 fusion.134
  1286.3 40.3 %all-reduce = (f32[4,1024]{1,0:T(4,128)}, f32[4,1024]{1,0:T(4,128)}, f32[3,1024]{1,0:T(4,128)}) all-reduce(f32[4,1024]{1,0:T(4,128)S(1)} %get-tuple-element.481, f32[4,1024]{1,0:T(4,128)S(1)} %get-tuple-element.482, f32[3,1024]{1,0:T(4,128)S(1)} %pad_maximum_fusion.2), channel_id=1, replica_groups=mesh['dp'=16,'tensor'=2] {'dp','tensor'}, use_global_device_ids=true, to_apply=%region_46.47 | all-reduce | flops 11264 | bytes 90112 | tf_op jit(solution)/shard_map/psum | solution.py:339
  1326.6 7.2 fusion.135
  (464 shorter events, 263.9 us)
Async XLA Ops:
  7.2 150.5 %copy-start = (bf16[1024,512]{1,0:T(8,128)(2,1)S(1)}, bf16[1024,512]{1,0:T(8,128)(2,1)}, u32[]{:S(2)}) copy-start(bf16[1024,512]{1,0:T(8,128)(2,1)} %param.36) | copy-start | bytes 3145732
  7.2 44.3 %all-gather.10.cloned.1.call-start = ((), (), s32[]{:S(2)}) async-start(), calls=%async_computation.8 | async-start | bytes 3145728 | tf_op jit(solution)/shard_map/all_gather | solution.py:234
  8.8 9.7 copy-start.68
  11.9 271.8 %copy-start.60 = (f32[1,1024]{1,0:T(1,128)}, f32[1,1024]{1,0:T(1,128)S(1)}, u32[]{:S(2)}) copy-start(f32[1,1024]{1,0:T(1,128)S(1)} %get-tuple-element.474) | copy-start | bytes 12292
  15.5 142.1 %all-gather.8.cloned.1.call-start = ((), (), s32[]{:S(2)}) async-start(), calls=%async_computation.7 | async-start | bytes 12582912 | tf_op jit(solution)/shard_map/all_gather | solution.py:235
  24.0 27.5 %copy-start.95 = (bf16[1024,512]{1,0:T(8,128)(2,1)S(1)}, bf16[1024,512]{1,0:T(8,128)(2,1)}, u32[]{:S(2)}) copy-start(bf16[1024,512]{1,0:T(8,128)(2,1)} %param.35) | copy-start | bytes 3145732
  24.0 257.0 %reduce-scatter.8.cloned.1.call-start = ((), (), s32[]{:S(2)}) async-start(), calls=%async_computation.9 | async-start | bytes 6291456 | tf_op jit(solution)/shard_map/reduce_scatter | solution.py:166
  226.5 91.8 %all-gather.12.cloned.1.call-start = ((), (), s32[]{:S(2)}) async-start(), calls=%async_computation.10 | async-start | bytes 3145728 | tf_op jit(solution)/shard_map/all_gather | solution.py:154
  283.3 140.1 %copy-start.8 = (f32[512,1024]{1,0:T(8,128)}, f32[512,1024]{1,0:T(8,128)S(1)}, u32[]{:S(2)}) copy-start(f32[512,1024]{1,0:T(8,128)S(1)} %get-tuple-element.451) | copy-start | bytes 6291460
  283.3 39.1 %copy-start.66 = (f32[512]{0:T(512)}, f32[512]{0:T(512)S(1)}, u32[]{:S(2)}) copy-start(f32[512]{0:T(512)S(1)} %broadcast_multiply_fusion.2) | copy-start | bytes 6148
  283.6 38.8 %copy-start.76 = (f32[512]{0:T(512)}, f32[512]{0:T(512)S(1)}, u32[]{:S(2)}) copy-start(f32[512]{0:T(512)S(1)} %multiply_reduce_fusion.3) | copy-start | bytes 6148
  283.7 38.7 %copy-start.70 = (f32[512]{0:T(512)}, f32[512]{0:T(512)S(1)}, u32[]{:S(2)}) copy-start(f32[512]{0:T(512)S(1)} %fusion.205) | copy-start | bytes 6148
  285.1 138.3 %reduce-scatter.10.cloned.1.call-start = ((), (), s32[]{:S(2)}) async-start(), calls=%async_computation.11 | async-start | bytes 6291456 | tf_op jit(solution)/shard_map/reduce_scatter | solution.py:166
  368.9 92.4 %all-gather.14.cloned.1.call-start = ((), (), s32[]{:S(2)}) async-start(), calls=%async_computation.12 | async-start | bytes 3145728 | tf_op jit(solution)/shard_map/all_gather | solution.py:154
  428.0 67.9 %all-gather.16.cloned.1.call-start = ((), (), s32[]{:S(2)}) async-start(), calls=%async_computation.14 | async-start | bytes 3145728 | tf_op jit(solution)/shard_map/all_gather | solution.py:158
  428.8 120.1 %reduce-scatter.14.cloned.1.call-start = ((), (), s32[]{:S(2)}) async-start(), calls=%async_computation.15 | async-start | bytes 3145728 | tf_op jit(solution)/shard_map/reduce_scatter | solution.py:175
  495.9 15.1 %copy-start.88 = (bf16[1024,2048]{1,0:T(8,128)(2,1)S(1)}, bf16[1024,2048]{1,0:T(8,128)(2,1)}, u32[]{:S(2)}) copy-start(bf16[1024,2048]{1,0:T(8,128)(2,1)} %param.43) | copy-start | bytes 12582916
  516.8 88.8 %reduce-scatter.12.cloned.1.call-start = ((), (), s32[]{:S(2)}) async-start(), calls=%async_computation.13 | async-start | bytes 6291456 | tf_op jit(solution)/shard_map/reduce_scatter | solution.py:166
  528.8 20.0 %copy-start.14 = (f32[512,1024]{1,0:T(8,128)S(1)}, f32[512,1024]{1,0:T(8,128)}, u32[]{:S(2)}) copy-start(f32[512,1024]{1,0:T(8,128)} %copy-done.13) | copy-start | bytes 6291460
  528.8 117.1 %all-gather.18.cloned.1.call-start = ((), (), s32[]{:S(2)}) async-start(), calls=%async_computation.16 | async-start | bytes 3145728 | tf_op jit(solution)/shard_map/all_gather | solution.py:158
  612.7 105.3 %reduce-scatter.16.cloned.1.call-start = ((), (), s32[]{:S(2)}) async-start(), calls=%async_computation.17 | async-start | bytes 3145728 | tf_op jit(solution)/shard_map/reduce_scatter | solution.py:175
  685.9 75.1 %all-gather.20.cloned.1.call-start = ((), (), s32[]{:S(2)}) async-start(), calls=%async_computation.18 | async-start | bytes 3145728 | tf_op jit(solution)/shard_map/all_gather | solution.py:158
  686.2 31.7 %copy-start.9 = (f32[512,1024]{1,0:T(8,128)S(1)}, f32[512,1024]{1,0:T(8,128)}, u32[]{:S(2)}) copy-start(f32[512,1024]{1,0:T(8,128)} %copy-done.8) | copy-start | bytes 6291460
  686.3 31.7 %copy-start.61 = (f32[1,1024]{1,0:T(1,128)S(1)}, f32[1,1024]{1,0:T(1,128)}, u32[]{:S(2)}) copy-start(f32[1,1024]{1,0:T(1,128)} %copy-done.60) | copy-start | bytes 12292
  686.3 31.7 %copy-start.67 = (f32[512]{0:T(512)S(1)}, f32[512]{0:T(512)}, u32[]{:S(2)}) copy-start(f32[512]{0:T(512)} %copy-done.66) | copy-start | bytes 6148
  686.3 34.4 %copy-start.77 = (f32[512]{0:T(512)S(1)}, f32[512]{0:T(512)}, u32[]{:S(2)}) copy-start(f32[512]{0:T(512)} %copy-done.76) | copy-start | bytes 6148
  686.3 34.4 %copy-start.71 = (f32[512]{0:T(512)S(1)}, f32[512]{0:T(512)}, u32[]{:S(2)}) copy-start(f32[512]{0:T(512)} %copy-done.70) | copy-start | bytes 6148
  727.8 10.1 copy-start.51
  727.8 188.8 %reduce-scatter.18.cloned.1.call-start = ((), (), s32[]{:S(2)}) async-start(), calls=%async_computation.19 | async-start | bytes 3145728 | tf_op jit(solution)/shard_map/reduce_scatter | solution.py:175
  742.4 18.6 %copy-start.94 = (bf16[512,1024]{1,0:T(8,128)(2,1)S(1)}, bf16[512,1024]{1,0:T(8,128)(2,1)}, u32[]{:S(2)}) copy-start(bf16[512,1024]{1,0:T(8,128)(2,1)} %param.38) | copy-start | bytes 3145732
  744.7 20.9 %copy-start.55 = (f32[2,4,4,128]{3,2,1,0:T(4,128)S(1)}, f32[2,4,4,128]{3,2,1,0:T(4,128)}, u32[]{:S(2)}) copy-start(f32[2,4,4,128]{3,2,1,0:T(4,128)} %copy-done.54) | copy-start | bytes 49156
  744.7 20.9 %copy-start.101 = (s32[2,4]{1,0:T(2,128)S(1)}, s32[2,4]{1,0:T(2,128)}, u32[]{:S(2)}) copy-start(s32[2,4]{1,0:T(2,128)} %copy-done.100) | copy-start | bytes 100
  833.9 339.1 %all-reduce.4.cloned.1.call-start = ((), (), s32[]{:S(2)}) async-start(), calls=%async_computation.21 | async-start | bytes 33554432 | tf_op jit(solution)/shard_map/psum | solution.py:355
  840.5 11.4 slice-start
  857.4 10.6 copy-start.97
  857.4 417.4 %reduce-scatter.20.cloned.1.call-start = ((), (), s32[]{:S(2)}) async-start(), calls=%async_computation.20 | async-start | bytes 12582912 | tf_op jit(solution)/shard_map/reduce_scatter | solution.py:184
  879.3 37.1 %copy-start.82 = (f32[1024]{0:T(1024)S(1)}, f32[1024]{0:T(1024)}, u32[]{:S(2)}) copy-start(f32[1024]{0:T(1024)} %get-tuple-element.444) | copy-start | bytes 12292
  879.3 37.1 %copy-start.83 = (f32[1024]{0:T(1024)S(1)}, f32[1024]{0:T(1024)}, u32[]{:S(2)}) copy-start(f32[1024]{0:T(1024)} %get-tuple-element.350) | copy-start | bytes 12292
  879.4 37.1 %copy-start.84 = (f32[1024]{0:T(1024)S(1)}, f32[1024]{0:T(1024)}, u32[]{:S(2)}) copy-start(f32[1024]{0:T(1024)} %get-tuple-element.351) | copy-start | bytes 12292
  879.4 37.2 %copy-start.16 = (bf16[512,1024]{1,0:T(8,128)(2,1)S(1)}, bf16[512,1024]{1,0:T(8,128)(2,1)}, u32[]{:S(2)}) copy-start(bf16[512,1024]{1,0:T(8,128)(2,1)} %param.29) | copy-start | bytes 3145732
  879.4 37.2 %copy-start.63 = (f32[1,1024]{1,0:T(1,128)S(1)}, f32[1,1024]{1,0:T(1,128)}, u32[]{:S(2)}) copy-start(f32[1,1024]{1,0:T(1,128)} %copy-done.62) | copy-start | bytes 12292
  879.4 37.2 %copy-start.69 = (f32[512]{0:T(512)S(1)}, f32[512]{0:T(512)}, u32[]{:S(2)}) copy-start(f32[512]{0:T(512)} %copy-done.68) | copy-start | bytes 6148
  879.4 39.2 %copy-start.75 = (f32[512]{0:T(512)S(1)}, f32[512]{0:T(512)}, u32[]{:S(2)}) copy-start(f32[512]{0:T(512)} %copy-done.74) | copy-start | bytes 6148
  879.4 39.3 %copy-start.73 = (f32[512]{0:T(512)S(1)}, f32[512]{0:T(512)}, u32[]{:S(2)}) copy-start(f32[512]{0:T(512)} %copy-done.72) | copy-start | bytes 6148
  1193.0 81.9 %copy-start.53 = (f32[2048]{0:T(1024)S(1)}, f32[2048]{0:T(1024)}, u32[]{:S(2)}) copy-start(f32[2048]{0:T(1024)} %copy-done.52) | copy-start | bytes 24580
  1193.0 81.9 %copy-start.59 = (f32[1,1024]{1,0:T(1,128)S(1)}, f32[1,1024]{1,0:T(1,128)}, u32[]{:S(2)}) copy-start(f32[1,1024]{1,0:T(1,128)} %copy-done.58) | copy-start | bytes 12292
  1197.4 83.3 %copy-start.65 = (f32[2048]{0:T(1024)S(1)}, f32[2048]{0:T(1024)}, u32[]{:S(2)}) copy-start(f32[2048]{0:T(1024)} %copy-done.64) | copy-start | bytes 24580
  1197.4 83.3 %copy-start.57 = (f32[2048]{0:T(1024)S(1)}, f32[2048]{0:T(1024)}, u32[]{:S(2)}) copy-start(f32[2048]{0:T(1024)} %copy-done.56) | copy-start | bytes 24580
  (88 other events, 334.7 us)
Sparse Core Ops, SparseCore 0:
  15.6 35.8 all-gather.9
  53.6 104.0 all-gather.7
  226.7 54.3 reduce-scatter.7
  285.2 33.0 all-gather.11
  369.0 54.3 reduce-scatter.9
  428.1 33.0 all-gather.13
  462.8 33.0 all-gather.15
  516.9 31.8 reduce-scatter.13
  551.1 54.3 reduce-scatter.11
  612.8 33.0 all-gather.17
  686.0 31.8 reduce-scatter.15
  727.9 33.0 all-gather.19
  834.0 31.8 reduce-scatter.17
  873.9 298.9 all-reduce.3
  1175.7 99.0 reduce-scatter.19
where the time goes:
time: 1350 us; the launch traced here: 1340 us
  waiting for transfers between devices  786 us (58%)
  matrix products  230 us (17%)
  local copies, waits for them, and re-layouts  137 us (10%)
  other arithmetic  93.8 us (7%)
  blocking collectives  76.1 us (6%)
  between operations  15.2 us (1%)
    psum x1, waiting for transfers between devices, shards(): lax.psum(d_cross_q.astype(jnp.bfloat16), 'dp').astype(jnp.float32)  250 us
    reduce_scatter x3, waiting for transfers between devices, branch_sum(): lax.psum_scatter(term(jnp.int32(0), lax.axis_size('tensor') * own_rows),...  162 us
    all_gather x1, waiting for transfers between devices, shards(): lax.all_gather(in_normed, 'tensor', axis=0, tiled=True)  102 us
    reduce_scatter x1, waiting for transfers between devices, back_inputs(): lax.psum_scatter(term(jnp.int32(0), own_rows * lax.axis_size('tensor')).a...  77.4 us
    dot_general x10, matrix products, matmul(): return jnp.dot(left, right, preferred_element_type=jnp.float32)  66.2 us
    all_gather x2, waiting for transfers between devices, gather_rows(): return lax.all_gather(normed, 'tensor', axis=0, tiled=True)  65.2 us
    all_gather x3, waiting for transfers between devices, gather_grads(): return lax.all_gather(grads, 'tensor', axis=0, tiled=True)  62.9 us
    dot_general x10, matrix products, times_transposed(): lax.dot_general(left, right, (((1,), (1,)), ((), ())), preferred_element_...  58.8 us
  transfers between devices with their start and end apart: 15, of which 14 were waited for; matrix products, arithmetic and copies ran while one was open for 11% of the time, Pallas kernels for 0%

commit v1 on v0

--- a/solution.py
+++ b/solution.py
@@ -10,6 +10,10 @@
 NEG_LARGE = -1e30
 GELU_COEF = 0.7978845608028654
 GELU_CUBE = 0.044715
+
+
+def pair_sides(mine_x):
+    return lax.all_gather(mine_x, "dp").sum(axis=0)
 
 
 def layer_norm(values, gain, shift):
@@ -352,7 +356,7 @@
         d_upb,
         d_down,
     ) = (
-        lax.psum(d_cross_q.astype(jnp.bfloat16), "dp").astype(jnp.float32),
+        pair_sides(d_cross_q.astype(jnp.bfloat16)).astype(jnp.float32),
         lax.psum(d_cross_k.astype(jnp.bfloat16), "dp").astype(jnp.float32),
         lax.psum(d_cross_v.astype(jnp.bfloat16), "dp").astype(jnp.float32),
         lax.psum(d_cross_o.astype(jnp.bfloat16), "dp").astype(jnp.float32),

time: 1350 us -> 1410 us (1.044)
  waiting for transfers between devices: 786 us -> 835 us
    all_gather x0 -> x1, waiting for transfers between devices: none -> 66.9 us  [pair_sides(): return lax.all_gather(mine_x, 'dp').sum(axis=0)]
    psum x1, waiting for transfers between devices: 250 us -> 227 us  [shards(): lax.psum(d_cross_k.astype(jnp.bfloat16), 'dp').astype(jnp.float32)]
  transfers between devices with their start and end apart: 15 -> 16, of which waited for: 14 -> 15; matrix products, arithmetic and copies ran while one was open for 11% -> 12% of each run, Pallas kernels for 0% -> 0%
where the time goes in v1:
time: 1410 us; the launch traced here: 1400 us
  waiting for transfers between devices  835 us (59%)
  matrix products  231 us (16%)
  local copies, waits for them, and re-layouts  138 us (10%)
  other arithmetic  103 us (7%)
  blocking collectives  78.8 us (6%)
  between operations  14.9 us (1%)
    psum x1, waiting for transfers between devices, shards(): lax.psum(d_cross_k.astype(jnp.bfloat16), 'dp').astype(jnp.float32)  227 us
    reduce_scatter x3, waiting for transfers between devices, branch_sum(): lax.psum_scatter(term(jnp.int32(0), lax.axis_size('tensor') * own_rows),...  162 us
    all_gather x1, waiting for transfers between devices, shards(): lax.all_gather(in_normed, 'tensor', axis=0, tiled=True)  102 us
    reduce_scatter x1, waiting for transfers between devices, back_inputs(): lax.psum_scatter(term(jnp.int32(0), own_rows * lax.axis_size('tensor')).a...  79.5 us
    all_gather x1, waiting for transfers between devices, pair_sides(): return lax.all_gather(mine_x, 'dp').sum(axis=0)  66.9 us
    dot_general x10, matrix products, matmul(): return jnp.dot(left, right, preferred_element_type=jnp.float32)  66.2 us
    all_gather x2, waiting for transfers between devices, gather_rows(): return lax.all_gather(normed, 'tensor', axis=0, tiled=True)  65.5 us
    all_gather x3, waiting for transfers between devices, gather_grads(): return lax.all_gather(grads, 'tensor', axis=0, tiled=True)  62.4 us
  transfers between devices with their start and end apart: 16, of which 15 were waited for; matrix products, arithmetic and copies ran while one was open for 12% of the time, Pallas kernels for 0%

profile of v1, /device:TPU:0, one launch (start us, length us, event | category | flops | bytes accessed | tf_op | source)
XLA Modules:
  0.0 1404.5 jit_solution(5708767779935764720)
XLA Ops:
  24.9 26.5 %all-gather.12.cloned.1.call-done = bf16[1024,1024]{1,0:T(8,128)(2,1)} async-done(((bf16[512,1024]{1,0:T(8,128)(2,1)}), bf16[1024,1024]{1,0:T(8,128)(2,1)}) %all-gather.12.cloned.1.call-update) | async-done | bytes 2097168 | tf_op jit(solution)/shard_map/all_gather | solution.py:238
  56.1 101.5 %all-gather.10.cloned.1.call-done = bf16[4096,1024]{1,0:T(8,128)(2,1)} async-done(((bf16[2048,1024]{1,0:T(8,128)(2,1)}), bf16[4096,1024]{1,0:T(8,128)(2,1)}) %all-gather.10.cloned.1.call-update) | async-done | bytes 8388624 | tf_op jit(solution)/shard_map/all_gather | solution.py:239
  157.6 9.4 convolution_convert_fusion.3
  167.0 6.9 reshape.380
  173.9 5.3 copy.124
  179.3 9.4 convolution_convert_fusion.4
  188.7 6.9 reshape.378
  196.8 24.9 %while.62 = (s32[]{:T(128)}, bf16[2,4,128,4,128]{4,3,2,1,0:T(4,128)(2,1)}, f32[2,4,4,128]{3,2,1,0:T(4,128)S(1)}, bf16[2,4,512,4,128]{4,3,2,1,0:T(4,128)(2,1)}, s...) while((s32[]{:T(128)}, ...), condition=%wide.region_8.9_spmd, body=%wide.region_5.8_spmd.sunk | while | flops 549715968 | bytes 45163760 | solution.py:101
  221.7 4.8 fusion.191
  227.2 53.8 %reduce-scatter.8.cloned.1.call-done = f32[512,1024]{1,0:T(8,128)} async-done(((f32[1024,1024]{1,0:T(8,128)}), f32[512,1024]{1,0:T(8,128)}) %reduce-scatter.8.cloned.1.call-update) | async-done | bytes 2097168 | tf_op jit(solution)/shard_map/reduce_scatter | solution.py:170
  285.1 33.2 %all-gather.14.cloned.1.call-done = bf16[1024,1024]{1,0:T(8,128)(2,1)} async-done(((bf16[512,1024]{1,0:T(8,128)(2,1)}), bf16[1024,1024]{1,0:T(8,128)(2,1)}) %all-gather.14.cloned.1.call-update) | async-done | bytes 2097168 | tf_op jit(solution)/shard_map/all_gather | solution.py:158
  345.3 18.6 %while.63 = (s32[]{:T(128)}, bf16[2,4,128,4,128]{4,3,2,1,0:T(4,128)(2,1)}, bf16[2,4,128,4,128]{2,4,3,1,0:T(8,128)(2,1)}, bf16[2,4,128,4,128]{4,2,3,1,0:T(8,128)(...) while((s32[]{:T(128)}, bf16[2,4,128,4,128]{4,3,2,1,0:T(4,128)(2,1)}, ...), condition=%wide.region_15.16_spmd, body=%wide.region_12.15_spmd.sunk | while | flops 136053376 | bytes 6309973 | solution.py:101
  364.0 4.8 fusion.187
  368.9 54.5 %reduce-scatter.10.cloned.1.call-done = f32[512,1024]{1,0:T(8,128)} async-done(((f32[1024,1024]{1,0:T(8,128)}), f32[512,1024]{1,0:T(8,128)}) %reduce-scatter.10.cloned.1.call-update) | async-done | bytes 2097168 | tf_op jit(solution)/shard_map/reduce_scatter | solution.py:170
  429.0 32.3 %all-gather.16.cloned.1.call-done = bf16[1024,1024]{1,0:T(8,128)(2,1)} async-done(((bf16[512,1024]{1,0:T(8,128)(2,1)}), bf16[1024,1024]{1,0:T(8,128)(2,1)}) %all-gather.16.cloned.1.call-update) | async-done | bytes 2097168 | tf_op jit(solution)/shard_map/all_gather | solution.py:158
  461.2 10.9 fusion.228
  472.1 23.8 %all-gather.18.cloned.1.call-done = bf16[1024,1024]{1,0:T(8,128)(2,1)} async-done(((bf16[512,1024]{1,0:T(8,128)(2,1)}), bf16[1024,1024]{1,0:T(8,128)(2,1)}) %all-gather.18.cloned.1.call-update) | async-done | bytes 2097168 | tf_op jit(solution)/shard_map/all_gather | solution.py:162
  495.9 13.1 fusion.227
  511.0 5.7 convolution_convert_fusion.8
  517.0 11.8 fusion.211
  528.9 19.9 %reduce-scatter.14.cloned.1.call-done = bf16[512,1024]{1,0:T(8,128)(2,1)} async-done(((bf16[1024,1024]{1,0:T(8,128)(2,1)}), bf16[512,1024]{1,0:T(8,128)(2,1)}) %reduce-scatter.14.cloned.1.call-update) | async-done | bytes 1048592 | tf_op jit(solution)/shard_map/reduce_scatter | solution.py:179
  551.4 54.1 %reduce-scatter.12.cloned.1.call-done = f32[512,1024]{1,0:T(8,128)} async-done(((f32[1024,1024]{1,0:T(8,128)}), f32[512,1024]{1,0:T(8,128)}) %reduce-scatter.12.cloned.1.call-update) | async-done | bytes 2097168 | tf_op jit(solution)/shard_map/reduce_scatter | solution.py:170
  614.2 8.9 while.64
  623.1 22.8 %all-gather.20.cloned.1.call-done = bf16[1024,1024]{1,0:T(8,128)(2,1)} async-done(((bf16[512,1024]{1,0:T(8,128)(2,1)}), bf16[1024,1024]{1,0:T(8,128)(2,1)}) %all-gather.20.cloned.1.call-update) | async-done | bytes 2097168 | tf_op jit(solution)/shard_map/all_gather | solution.py:162
  655.9 22.7 %while.65 = (s32[]{:T(128)}, bf16[2,4,128,4,128]{4,3,2,1,0:T(4,128)(2,1)}, bf16[2,4,128,4,128]{4,3,2,1,0:T(4,128)(2,1)}, bf16[2,4,128,4,128]{4,3,2,1,0:T(4,128)(...) while((s32[]{:T(128)}, ...), condition=%wide.region_29.30_spmd, body=%wide.region_27.29_spmd.sunk | while | flops 339212800 | bytes 40413460 | solution.py:149
  686.4 9.5 convolution_convert_fusion.6
  695.9 22.0 %reduce-scatter.16.cloned.1.call-done = bf16[512,1024]{1,0:T(8,128)(2,1)} async-done(((bf16[1024,1024]{1,0:T(8,128)(2,1)}), bf16[512,1024]{1,0:T(8,128)(2,1)}) %reduce-scatter.16.cloned.1.call-update) | async-done | bytes 1048592 | tf_op jit(solution)/shard_map/reduce_scatter | solution.py:179
  727.9 12.6 convolution_convert_fusion.5
  745.1 15.9 %all-gather.22.cloned.1.call-done = bf16[1024,1024]{1,0:T(8,128)(2,1)} async-done(((bf16[512,1024]{1,0:T(8,128)(2,1)}), bf16[1024,1024]{1,0:T(8,128)(2,1)}) %all-gather.22.cloned.1.call-update) | async-done | bytes 2097168 | tf_op jit(solution)/shard_map/all_gather | solution.py:162
  765.5 64.1 %while.66 = (s32[]{:T(128)}, bf16[2,4,128,4,128]{4,3,2,1,0:T(4,128)(2,1)}, bf16[2,4,512,4,128]{4,3,2,1,0:T(4,128)(2,1)}, bf16[2,4,512,4,128]{4,3,2,1,0:T(4,128)(...) while((s32[]{:T(128)}, ...), condition=%wide.region_35.36_spmd, body=%wide.region_33.35_spmd.sunk | while | flops 1361575936 | bytes 150537648 | solution.py:149
  777.7 4.7 multiply_reduce_fusion.7
  791.8 5.8 constant_dynamic-update-slice_fusion.18
  809.8 4.7 multiply_reduce_fusion.7
  823.8 5.8 constant_dynamic-update-slice_fusion.18
  844.0 8.3 fusion.171
  852.3 5.5 fusion.168
  857.9 10.5 fusion.142
  868.4 11.7 add_convert_fusion
  885.3 34.9 %psum.102 = bf16[2048]{0:T(1024)(128)(2,1)S(1)} all-reduce(bf16[2048]{0:T(1024)(128)(2,1)S(1)} %copy-done.78), channel_id=1, replica_groups=mesh['dp'=16,'tensor'=2] {'dp'}, use_global_device_ids=true, to_apply=%region_66.67 | all-reduce | flops 2048 | bytes 8192 | tf_op jit(solution)/shard_map/psum | solution.py:368
  927.6 227.3 %all-reduce.4.cloned.1.call-done = (bf16[1024,512]{1,0:T(8,128)(2,1)}, bf16[1024,512]{1,0:T(8,128)(2,1)}, bf16[512,1024]{1,0:T(8,128)(2,1)}, bf16[1024,512]{1,0:...) async-done(((bf16[1024,512]{1,0:T(8,128)(2,1)}, ...) | async-done | bytes 15728656 | tf_op jit(solution)/shard_map/psum | solution.py:360
  1168.8 4.4 convert_element_type.279
  1177.7 79.5 %reduce-scatter.20.cloned.1.call-done = bf16[2048,1024]{1,0:T(8,128)(2,1)} async-done(((bf16[4096,1024]{1,0:T(8,128)(2,1)}), bf16[2048,1024]{1,0:T(8,128)(2,1)}) %reduce-scatter.20.cloned.1.call-update) | async-done | bytes 4194320 | tf_op jit(solution)/shard_map/reduce_scatter | solution.py:188
  1257.2 5.7 convert_reduce_fusion
  1263.1 5.4 fusion.134
  1268.6 43.9 %all-reduce = (f32[4,1024]{1,0:T(4,128)}, f32[4,1024]{1,0:T(4,128)}, f32[3,1024]{1,0:T(4,128)}) all-reduce(f32[4,1024]{1,0:T(4,128)S(1)} %get-tuple-element.480, f32[4,1024]{1,0:T(4,128)S(1)} %get-tuple-element.481, f32[3,1024]{1,0:T(4,128)S(1)} %pad_maximum_fusion.2), channel_id=1, replica_groups=mesh['dp'=16,'tensor'=2] {'dp','tensor'}, use_global_device_ids=true, to_apply=%region_46.47 | all-reduce | flops 11264 | bytes 90112 | tf_op jit(solution)/shard_map/psum | solution.py:343
  1312.5 7.9 fusion.135
  1320.4 66.9 %all-gather.24.cloned.1.call-done = bf16[16384,512]{1,0:T(8,128)(2,1)} async-done(((bf16[1024,512]{1,0:T(8,128)(2,1)}), bf16[16384,512]{1,0:T(8,128)(2,1)}) %all-gather.24.cloned.1.call-update) | async-done | bytes 16777232 | tf_op jit(solution)/shard_map/all_gather | solution.py:16
  1387.3 8.9 reduce_sum.370
  (450 shorter events, 276.0 us)
Async XLA Ops:
  7.2 150.5 %copy-start = (bf16[1024,512]{1,0:T(8,128)(2,1)S(1)}, bf16[1024,512]{1,0:T(8,128)(2,1)}, u32[]{:S(2)}) copy-start(bf16[1024,512]{1,0:T(8,128)(2,1)} %param.36) | copy-start | bytes 3145732
  7.2 44.2 %all-gather.12.cloned.1.call-start = ((), (), s32[]{:S(2)}) async-start(), calls=%async_computation.8 | async-start | bytes 3145728 | tf_op jit(solution)/shard_map/all_gather | solution.py:238
  8.8 9.7 copy-start.63
  11.9 8.5 copy-start.59
  11.9 8.5 copy-start.57
  15.5 142.1 %all-gather.10.cloned.1.call-start = ((), (), s32[]{:S(2)}) async-start(), calls=%async_computation.7 | async-start | bytes 12582912 | tf_op jit(solution)/shard_map/all_gather | solution.py:239
  24.0 27.5 %copy-start.86 = (bf16[1024,512]{1,0:T(8,128)(2,1)S(1)}, bf16[1024,512]{1,0:T(8,128)(2,1)}, u32[]{:S(2)}) copy-start(bf16[1024,512]{1,0:T(8,128)(2,1)} %param.35) | copy-start | bytes 3145732
  24.0 257.0 %reduce-scatter.8.cloned.1.call-start = ((), (), s32[]{:S(2)}) async-start(), calls=%async_computation.9 | async-start | bytes 6291456 | tf_op jit(solution)/shard_map/reduce_scatter | solution.py:170
  226.5 91.8 %all-gather.14.cloned.1.call-start = ((), (), s32[]{:S(2)}) async-start(), calls=%async_computation.10 | async-start | bytes 3145728 | tf_op jit(solution)/shard_map/all_gather | solution.py:158
  283.3 140.1 %copy-start.8 = (f32[512,1024]{1,0:T(8,128)}, f32[512,1024]{1,0:T(8,128)S(1)}, u32[]{:S(2)}) copy-start(f32[512,1024]{1,0:T(8,128)S(1)} %get-tuple-element.450) | copy-start | bytes 6291460
  285.1 138.3 %reduce-scatter.10.cloned.1.call-start = ((), (), s32[]{:S(2)}) async-start(), calls=%async_computation.11 | async-start | bytes 6291456 | tf_op jit(solution)/shard_map/reduce_scatter | solution.py:170
  368.8 92.4 %all-gather.16.cloned.1.call-start = ((), (), s32[]{:S(2)}) async-start(), calls=%async_computation.12 | async-start | bytes 3145728 | tf_op jit(solution)/shard_map/all_gather | solution.py:158
  428.0 67.9 %all-gather.18.cloned.1.call-start = ((), (), s32[]{:S(2)}) async-start(), calls=%async_computation.14 | async-start | bytes 3145728 | tf_op jit(solution)/shard_map/all_gather | solution.py:162
  428.7 120.0 %reduce-scatter.14.cloned.1.call-start = ((), (), s32[]{:S(2)}) async-start(), calls=%async_computation.15 | async-start | bytes 3145728 | tf_op jit(solution)/shard_map/reduce_scatter | solution.py:179
  495.9 15.1 %copy-start.79 = (bf16[1024,2048]{1,0:T(8,128)(2,1)S(1)}, bf16[1024,2048]{1,0:T(8,128)(2,1)}, u32[]{:S(2)}) copy-start(bf16[1024,2048]{1,0:T(8,128)(2,1)} %param.43) | copy-start | bytes 12582916
  516.7 88.8 %reduce-scatter.12.cloned.1.call-start = ((), (), s32[]{:S(2)}) async-start(), calls=%async_computation.13 | async-start | bytes 6291456 | tf_op jit(solution)/shard_map/reduce_scatter | solution.py:170
  528.8 20.0 %copy-start.14 = (f32[512,1024]{1,0:T(8,128)S(1)}, f32[512,1024]{1,0:T(8,128)}, u32[]{:S(2)}) copy-start(f32[512,1024]{1,0:T(8,128)} %copy-done.13) | copy-start | bytes 6291460
  528.8 117.1 %all-gather.20.cloned.1.call-start = ((), (), s32[]{:S(2)}) async-start(), calls=%async_computation.16 | async-start | bytes 3145728 | tf_op jit(solution)/shard_map/all_gather | solution.py:162
  612.6 105.3 %reduce-scatter.16.cloned.1.call-start = ((), (), s32[]{:S(2)}) async-start(), calls=%async_computation.17 | async-start | bytes 3145728 | tf_op jit(solution)/shard_map/reduce_scatter | solution.py:179
  685.8 75.1 %all-gather.22.cloned.1.call-start = ((), (), s32[]{:S(2)}) async-start(), calls=%async_computation.18 | async-start | bytes 3145728 | tf_op jit(solution)/shard_map/all_gather | solution.py:162
  686.4 31.5 %copy-start.9 = (f32[512,1024]{1,0:T(8,128)S(1)}, f32[512,1024]{1,0:T(8,128)}, u32[]{:S(2)}) copy-start(f32[512,1024]{1,0:T(8,128)} %copy-done.8) | copy-start | bytes 6291460
  727.7 12.9 copy-start.49
  727.7 193.2 %reduce-scatter.18.cloned.1.call-start = ((), (), s32[]{:S(2)}) async-start(), calls=%async_computation.19 | async-start | bytes 3145728 | tf_op jit(solution)/shard_map/reduce_scatter | solution.py:179
  727.9 12.6 copy-start.82
  742.8 18.1 %copy-start.85 = (bf16[512,1024]{1,0:T(8,128)(2,1)S(1)}, bf16[512,1024]{1,0:T(8,128)(2,1)}, u32[]{:S(2)}) copy-start(bf16[512,1024]{1,0:T(8,128)(2,1)} %param.38) | copy-start | bytes 3145732
  745.0 20.5 %copy-start.54 = (f32[2,4,4,128]{3,2,1,0:T(4,128)S(1)}, f32[2,4,4,128]{3,2,1,0:T(4,128)}, u32[]{:S(2)}) copy-start(f32[2,4,4,128]{3,2,1,0:T(4,128)} %copy-done.53) | copy-start | bytes 49156
  745.0 20.5 %copy-start.92 = (s32[2,4]{1,0:T(2,128)S(1)}, s32[2,4]{1,0:T(2,128)}, u32[]{:S(2)}) copy-start(s32[2,4]{1,0:T(2,128)} %copy-done.91) | copy-start | bytes 100
  765.8 6.1 copy-start.7
  833.9 321.0 %all-reduce.4.cloned.1.call-start = ((), (), s32[]{:S(2)}) async-start(), calls=%async_computation.22 | async-start | bytes 31457280 | tf_op jit(solution)/shard_map/psum | solution.py:360
  838.4 13.9 slice-start
  844.0 8.3 slice-start.1
  844.0 8.3 copy-start.81
  857.8 10.6 copy-start.88
  857.8 399.3 %reduce-scatter.20.cloned.1.call-start = ((), (), s32[]{:S(2)}) async-start(), calls=%async_computation.20 | async-start | bytes 12582912 | tf_op jit(solution)/shard_map/reduce_scatter | solution.py:188
  880.1 40.6 %copy-start.73 = (f32[1024]{0:T(1024)S(1)}, f32[1024]{0:T(1024)}, u32[]{:S(2)}) copy-start(f32[1024]{0:T(1024)} %get-tuple-element.443) | copy-start | bytes 12292
  880.1 40.6 %copy-start.74 = (f32[1024]{0:T(1024)S(1)}, f32[1024]{0:T(1024)}, u32[]{:S(2)}) copy-start(f32[1024]{0:T(1024)} %get-tuple-element.350) | copy-start | bytes 12292
  880.2 40.6 %copy-start.75 = (f32[1024]{0:T(1024)S(1)}, f32[1024]{0:T(1024)}, u32[]{:S(2)}) copy-start(f32[1024]{0:T(1024)} %get-tuple-element.351) | copy-start | bytes 12292
  880.2 40.7 %copy-start.16 = (bf16[512,1024]{1,0:T(8,128)(2,1)S(1)}, bf16[512,1024]{1,0:T(8,128)(2,1)}, u32[]{:S(2)}) copy-start(bf16[512,1024]{1,0:T(8,128)(2,1)} %param.29) | copy-start | bytes 3145732
  880.2 40.7 %copy-start.60 = (f32[1,1024]{1,0:T(1,128)S(1)}, f32[1,1024]{1,0:T(1,128)}, u32[]{:S(2)}) copy-start(f32[1,1024]{1,0:T(1,128)} %copy-done.59) | copy-start | bytes 12292
  880.2 40.7 %copy-start.64 = (f32[512]{0:T(512)S(1)}, f32[512]{0:T(512)}, u32[]{:S(2)}) copy-start(f32[512]{0:T(512)} %copy-done.63) | copy-start | bytes 6148
  880.2 42.8 %copy-start.68 = (f32[512]{0:T(512)S(1)}, f32[512]{0:T(512)}, u32[]{:S(2)}) copy-start(f32[512]{0:T(512)} %copy-done.67) | copy-start | bytes 6148
  880.2 42.8 %copy-start.66 = (f32[512]{0:T(512)S(1)}, f32[512]{0:T(512)}, u32[]{:S(2)}) copy-start(f32[512]{0:T(512)} %copy-done.65) | copy-start | bytes 6148
  880.2 507.1 %all-gather.24.cloned.1.call-start = ((), (), s32[]{:S(2)}) async-start(), calls=%async_computation.21 | async-start | bytes 17825792 | tf_op jit(solution)/shard_map/all_gather | solution.py:16
  1154.9 7.5 copy-start.41
  1173.2 83.9 %copy-start.52 = (f32[2048]{0:T(1024)S(1)}, f32[2048]{0:T(1024)}, u32[]{:S(2)}) copy-start(f32[2048]{0:T(1024)} %copy-done.51) | copy-start | bytes 24580
  1173.2 83.9 %copy-start.58 = (f32[1,1024]{1,0:T(1,128)S(1)}, f32[1,1024]{1,0:T(1,128)}, u32[]{:S(2)}) copy-start(f32[1,1024]{1,0:T(1,128)} %copy-done.57) | copy-start | bytes 12292
  1177.7 85.3 %copy-start.62 = (f32[2048]{0:T(1024)S(1)}, f32[2048]{0:T(1024)}, u32[]{:S(2)}) copy-start(f32[2048]{0:T(1024)} %copy-done.61) | copy-start | bytes 24580
  1177.7 85.3 %copy-start.56 = (f32[2048]{0:T(1024)S(1)}, f32[2048]{0:T(1024)}, u32[]{:S(2)}) copy-start(f32[2048]{0:T(1024)} %copy-done.55) | copy-start | bytes 24580
  (80 other events, 268.0 us)
Sparse Core Ops, SparseCore 0:
  15.6 35.8 all-gather.11
  53.6 104.0 all-gather.9
  226.7 54.3 reduce-scatter.7
  285.2 33.0 all-gather.13
  368.9 54.3 reduce-scatter.9
  428.1 33.0 all-gather.15
  462.8 33.0 all-gather.17
  516.8 31.8 reduce-scatter.13
  551.1 54.3 reduce-scatter.11
  612.8 33.0 all-gather.19
  686.0 31.8 reduce-scatter.15
  727.8 33.0 all-gather.21
  834.0 31.8 reduce-scatter.17
  873.6 281.2 all-reduce.3
  1157.6 99.5 reduce-scatter.19
  1259.8 127.4 all-gather.23
